TPU v7x, 512 devices: a whole 4x4x16 slice. The times are simulated.
512 devices in a mesh: dp: 2 (over y_lo), tensor: 4 (over x), context: 64 (over z, y_hi, core).
Axes of the slice: x: 4, y: 4 (y_hi: 2, y_lo: 2; y = y_hi * 2 + y_lo), z: 16, core: 2. Of those that a mesh axis runs over, the one named last changes fastest.
Arguments:
- q_in: bfloat16 [2, 8192, 4096], P('dp', 'context', 'tensor'), may hold values from -44 to 44
- k_in: bfloat16 [2, 8192, 4096], P('dp', 'context', 'tensor'), may hold values from -6 to 6
- v_in: bfloat16 [2, 8192, 4096], P('dp', 'context', 'tensor'), may hold values from -6 to 6
- short_filt: float32 [3, 7, 4096], P(None, None, 'tensor'), may hold values from -2 to 2
- long_filt: float32 [8192, 4096], P('context', 'tensor'), may hold values from -1.1 to 1.1
- norm_gain: float32 [4096], P('tensor'), may hold values from 0.1 to 1.9
- grad_out: bfloat16 [2, 8192, 4096], P('dp', 'context', 'tensor'), may hold values from -6 to 6
Outputs:
- mixed: bfloat16 [2, 8192, 4096], P('dp', 'context', 'tensor')
- grad_inputs: bfloat16 [3, 2, 8192, 4096], P(None, 'dp', 'context', 'tensor')
- grad_long: float32 [8192, 4096], P('context', 'tensor')
- grad_short: float32 [3, 7, 4096], P(None, None, 'tensor')
All inputs are finite; a program needn't handle non-finite values.
Results may differ from a plain program's by a relative error of at most 0.00225.
Values may be sent and summed in bfloat16 or wider, within the bound.
No kernel may reach another device: no remote copies, remote signals or barrier semaphores. Data moves between devices by JAX's collectives and lax.ppermute only.
A program may use at most 128 MiB of HBM per device.

v0:
```python
import math
import jax
import jax.numpy as jnp
from jax import lax
from jax.sharding import PartitionSpec as P

D = 4096
FILT = 7
EPS = 1e-06
HIGH = lax.Precision.HIGHEST


def passed_along(shard, axis, by):
    peers = lax.axis_size(axis)
    pairs = [(i, i + by) for i in range(peers) if 0 <= i + by < peers]
    return lax.ppermute(shard, axis, pairs)


def phases(first, second, modulus):
    product = first[:, None] * second[None, :] % modulus
    return product.astype(jnp.float32) * (2.0 * math.pi / modulus)


def block_table(block_len, sign):
    index = jnp.arange(block_len, dtype=jnp.int32)
    angle = phases(index, index, block_len)
    cosine = jnp.cos(angle)
    sine = jnp.sin(angle) * sign
    return jnp.stack([jnp.stack([cosine, sine]), jnp.stack([-sine, cosine])])


def forward_rows(values, modulus):
    count, block_len, width = values.shape
    ctx_size = lax.axis_size("context")
    sub_len = block_len // ctx_size
    spread = lax.all_to_all(
        values.reshape(count, 1, block_len, width),
        "context",
        split_axis=2,
        concat_axis=1,
        tiled=True,
    )
    freq = jnp.arange(2 * ctx_size, dtype=jnp.int32)
    place = (
        jnp.arange(ctx_size, dtype=jnp.int32)[:, None] * block_len
        + lax.axis_index("context") * sub_len
        + jnp.arange(sub_len, dtype=jnp.int32)[None, :]
    )
    angle = (freq[:, None, None] * place[None] % modulus).astype(jnp.float32) * (
        2.0 * math.pi / modulus
    )
    table = jnp.stack([jnp.cos(angle), -jnp.sin(angle)])
    turned = jnp.einsum("pkcs,ncsx->npksx", table, spread, precision=HIGH)
    moved = lax.all_to_all(turned, "context", split_axis=2, concat_axis=3, tiled=True)
    return jnp.einsum("pqmb,nqjbx->npjmx", block_table(block_len, 1.0), moved, precision=HIGH)


def inverse_rows(spec, modulus):
    rows = spec.shape[2]
    block_len = spec.shape[3]
    ctx_size = lax.axis_size("context")
    index = jnp.arange(block_len, dtype=jnp.int32)
    freq = 2 * lax.axis_index("context") + jnp.arange(rows, dtype=jnp.int32)
    total = freq[:, None, None] + 2 * ctx_size * index[None, :, None]
    angle = (total * index[None, None, :] % modulus).astype(jnp.float32) * (2.0 * math.pi / modulus)
    cosine = jnp.cos(angle)
    sine = jnp.sin(angle)
    table = jnp.stack([jnp.stack([cosine, -sine]), jnp.stack([sine, cosine])])
    turned = jnp.einsum("pqjmb,nqjmx->npjbx", table, spec, precision=HIGH)
    moved = lax.all_to_all(turned, "context", split_axis=3, concat_axis=2, tiled=True)
    outer = phases(
        jnp.arange(ctx_size, dtype=jnp.int32),
        jnp.arange(2 * ctx_size, dtype=jnp.int32),
        2 * ctx_size,
    )
    real_table = jnp.stack([jnp.cos(outer), -jnp.sin(outer)])
    values = jnp.einsum("qck,nqksx->ncsx", real_table, moved, precision=HIGH) / modulus
    back = lax.all_to_all(values, "context", split_axis=1, concat_axis=2, tiled=True)
    return back.reshape(back.shape[0], back.shape[2], back.shape[3])


def shards(q_in, k_in, v_in, short_filt, long_filt, norm_gain, grad_out):
    block_len = q_in.shape[1]
    channels = q_in.shape[2]
    edge_rows = FILT - 1
    modulus = 2 * lax.axis_size("context") * block_len
    branches = jnp.stack([q_in[0], k_in[0], v_in[0]])
    before = passed_along(branches[:, block_len - edge_rows :], "context", 1)
    inputs = jnp.concatenate([before, branches], 1).astype(jnp.float32)
    shorts = jnp.zeros((3, block_len, channels), jnp.float32)
    for lag in range(FILT):
        shorts = (
            shorts
            + short_filt[:, lag][:, None, :]
            * inputs[:, edge_rows - lag : edge_rows - lag + block_len]
        )
    q_short = shorts[0]
    k_short = shorts[1]
    v_short = shorts[2]
    kv_prod = k_short * v_short
    spectra = forward_rows(jnp.stack([kv_prod, long_filt]), modulus)
    kv_real, kv_imag = (spectra[0, 0], spectra[0, 1])
    filt_real, filt_imag = (spectra[1, 0], spectra[1, 1])
    conv_spec = jnp.stack(
        [kv_real * filt_real - kv_imag * filt_imag, kv_real * filt_imag + kv_imag * filt_real]
    )[None]
    conv = inverse_rows(conv_spec, modulus)[0]
    y_out = q_short * conv
    squares = lax.psum(jnp.sum(y_out * y_out, axis=-1), "tensor")
    rms = jnp.sqrt(squares / D + EPS)[:, None]
    mixed = (y_out / rms * norm_gain).astype(jnp.bfloat16)[None]
    grad_z = grad_out[0].astype(jnp.float32) * norm_gain
    prods = lax.psum(jnp.sum(grad_z * y_out, axis=-1), "tensor")[:, None]
    grad_y = grad_z / rms - y_out * prods / (D * rms**3)
    dconv = grad_y * q_short
    grad_q = grad_y * conv
    grad_spec = forward_rows(dconv[None], modulus)[0]
    grad_real = grad_spec[0]
    grad_imag = grad_spec[1]
    dkv_spec = jnp.stack(
        [
            filt_real * grad_real + filt_imag * grad_imag,
            filt_real * grad_imag - filt_imag * grad_real,
        ]
    )
    dfilt_spec = jnp.stack(
        [kv_real * grad_real + kv_imag * grad_imag, kv_real * grad_imag - kv_imag * grad_real]
    )
    results = inverse_rows(jnp.stack([dkv_spec, dfilt_spec]), modulus)
    dkv = results[0]
    dfilt_local = results[1]
    grads = jnp.stack([grad_q, dkv * v_short, dkv * k_short])
    after = passed_along(grads[:, :edge_rows].astype(jnp.bfloat16), "context", -1).astype(
        jnp.float32
    )
    extended = jnp.concatenate([grads, after], 1)
    grad_inputs = jnp.zeros((3, block_len, channels), jnp.float32)
    for lag in range(FILT):
        grad_inputs = (
            grad_inputs + short_filt[:, lag][:, None, :] * extended[:, lag : lag + block_len]
        )
    short_local = jnp.stack(
        [
            jnp.sum(grads * inputs[:, edge_rows - lag : edge_rows - lag + block_len], axis=1)
            for lag in range(FILT)
        ],
        1,
    )
    scale = 1.0 / math.sqrt(lax.axis_size("dp") * block_len * lax.axis_size("context"))
    grad_long = lax.psum(dfilt_local, "dp") * scale
    grad_short = lax.psum(short_local, ("dp", "context")) * scale
    return (mixed, grad_inputs.astype(jnp.bfloat16)[:, None], grad_long, grad_short)


def solution(mesh):
    in_specs = (
        P("dp", "context", "tensor"),
        P("dp", "context", "tensor"),
        P("dp", "context", "tensor"),
        P(None, None, "tensor"),
        P("context", "tensor"),
        P("tensor"),
        P("dp", "context", "tensor"),
    )
    out_specs = (
        P("dp", "context", "tensor"),
        P(None, "dp", "context", "tensor"),
        P("context", "tensor"),
        P(None, None, "tensor"),
    )
    return jax.shard_map(shards, mesh=mesh, in_specs=in_specs, out_specs=out_specs, check_vma=False)
```

profile of v0, /device:TPU:1, one launch (start us, length us, event | category | flops | bytes accessed | tf_op | source)
XLA Modules:
  0.0 1352.6 jit_solution(16455876887592393104)
XLA Ops:
  7.2 1.4 copy.63
  8.6 1.4 copy.64
  10.0 1.4 copy.65
  11.4 6.2 collective-permute-start
  18.2 2.1 collective-permute-done
  20.3 1.9 maximum_convert_fusion
  22.3 3.9 multiply_add_fusion
  26.2 1.4 copy-done.2
  27.6 1.8 fusion.95
  29.3 1.9 maximum_bitcast_fusion.4
  31.3 17.8 %all-to-all-start = ((f32[2,1,128,1024]{3,0,1,2:T(2,128)}), f32[2,1,128,1024]{3,0,1,2:T(2,128)S(1)}, u32[]{:S(2)}, u32[]{:S(2)}) async-start(f32[2,1,128,1024]{3,0,1,2:T(2,128)} %maximum_bitcast_fusion.4), calls=%async_computation | async-start | bytes 2097152 | tf_op jit(solution)/shard_map/all_to_all | solution.py:36
  49.5 53.7 %all-to-all-done = f32[2,1,128,1024]{3,0,1,2:T(2,128)S(1)} async-done(((f32[2,1,128,1024]{3,0,1,2:T(2,128)}), f32[2,1,128,1024]{3,0,1,2:T(2,128)S(1)}, u32[]{:S(2)}, u32[]{:S(2)}) %all-to-all-start) | async-done | bytes 1048608 | tf_op jit(solution)/shard_map/all_to_all | solution.py:36
  103.1 5.2 convolution_bitcast_fusion
  108.3 7.3 copy.68
  115.6 7.8 all-to-all-start.1
  124.8 184.3 %all-to-all-done.1 = f32[2,2,128,2,1024]{4,1,0,3,2:T(2,128)} async-done(((f32[2,2,128,2,1024]{4,1,0,3,2:T(2,128)}), f32[2,2,128,2,1024]{4,1,0,3,2:T(2,128)}, u32[]{:S(2)}, u32[]{:S(2)}) %all-to-all-start.1) | async-done | bytes 4194336 | tf_op jit(solution)/shard_map/all_to_all | solution.py:54
  309.1 5.4 copy.70
  314.5 8.1 fusion.4
  322.9 1.7 copy-done
  324.6 3.3 fusion.21
  328.0 4.2 copy.79
  332.2 10.6 all-to-all-start.2
  343.0 98.5 %all-to-all-done.2 = f32[1,2,2,128,1024]{4,1,2,0,3:T(2,128)} async-done(((f32[1,2,2,128,1024]{4,1,2,0,3:T(2,128)}), f32[1,2,2,128,1024]{4,1,2,0,3:T(2,128)}, u32[]{:S(2)}, u32[]{:S(2)}) %all-to-all-start.2) | async-done | bytes 2097184 | tf_op jit(solution)/shard_map/all_to_all | solution.py:70
  441.4 2.7 copy.80
  444.1 2.2 copy.81
  446.3 3.7 reshape.785
  450.0 3.1 fusion.30
  454.3 7.7 all-to-all-start.3
  463.2 32.8 %all-to-all-done.3 = f32[1,64,2,1024]{3,2,0,1:T(2,128)S(1)} async-done(((f32[1,64,2,1024]{3,2,0,1:T(2,128)}), f32[1,64,2,1024]{3,2,0,1:T(2,128)S(1)}, u32[]{:S(2)}, u32[]{:S(2)}) %all-to-all-start.3) | async-done | bytes 524320 | tf_op jit(solution)/shard_map/all_to_all | solution.py:78
  497.2 2.2 fusion.44
  499.4 9.3 all-reduce
  509.9 1.6 squeeze_reshape.9
  511.5 3.0 fusion.48
  514.5 40.9 %all_to_all.105 = f32[1,1,128,1024]{3,0,1,2:T(1,128)} all-to-all(f32[1,1,128,1024]{3,0,1,2:T(1,128)S(1)} %fusion.48), channel_id=1, replica_groups=mesh['dp'=2,'tensor'=4,'context'=64] {'context'}, dimensions={2} | all-to-all | bytes 1048576 | tf_op jit(solution)/shard_map/all_to_all | solution.py:36
  555.4 3.1 reduce
  558.5 2.1 reshape.786
  560.6 4.3 convolution_bitcast_fusion.1
  564.9 4.2 copy.86
  569.1 103.5 %all_to_all.106 = f32[1,2,128,2,1024]{4,1,3,0,2:T(2,128)S(1)} all-to-all(f32[1,2,128,2,1024]{4,1,3,0,2:T(2,128)} %copy.86), channel_id=1, replica_groups=mesh['dp'=2,'tensor'=4,'context'=64] {'context'}, dimensions={2} | all-to-all | bytes 4194304 | tf_op jit(solution)/shard_map/all_to_all | solution.py:54
  673.7 2.5 copy.88
  676.2 4.1 copy.89
  680.3 3.6 fusion.24
  684.8 5.0 fusion.7
  689.7 7.3 copy.95
  697.1 196.5 %all_to_all.107 = f32[2,2,2,128,1024]{4,1,0,2,3:T(2,128)S(1)} all-to-all(f32[2,2,2,128,1024]{4,1,0,2,3:T(2,128)} %copy.95), channel_id=1, replica_groups=mesh['dp'=2,'tensor'=4,'context'=64] {'context'}, dimensions={3} | all-to-all | bytes 8388608 | tf_op jit(solution)/shard_map/all_to_all | solution.py:70
  893.6 5.3 copy.97
  898.8 6.0 all_to_all.95
  904.9 4.6 fusion.28
  909.5 1.8 copy.98
  911.2 8.2 all-to-all-start.7
  919.5 1.6 squeeze_reshape.7
  921.1 52.3 %all-to-all-done.7 = f32[2,64,2,1024]{3,2,0,1:T(2,128)} async-done(((f32[2,64,2,1024]{3,2,0,1:T(2,128)}), f32[2,64,2,1024]{3,2,0,1:T(2,128)}, u32[]{:S(2)}, u32[]{:S(2)}) %all-to-all-start.7) | async-done | bytes 1048608 | tf_op jit(solution)/shard_map/all_to_all | solution.py:78
  973.4 2.1 fusion.96
  975.5 1.6 squeeze.10
  977.1 7.5 fusion.41
  984.6 4.3 multiply_reduce_fusion
  990.1 2.5 pad_maximum_fusion.1
  992.6 4.4 collective-permute-start.1
  999.2 2.3 collective-permute-done.1
  1001.5 2.5 pad_maximum_fusion
  1004.1 3.8 fusion.40
  1009.0 289.3 %all-reduce.6.cloned.1.call-done = f32[3,7,1024]{2,0,1:T(4,128)} async-done(((f32[3,7,1024]{2,0,1:T(4,128)}), f32[3,7,1024]{2,0,1:T(4,128)}) %all-reduce.6.cloned.1.call-update) | async-done | bytes 86032 | tf_op jit(solution)/shard_map/psum | solution.py:151
  1299.9 43.4 %all-reduce.4.cloned.1.call-done = f32[128,1024]{1,0:T(8,128)} async-done(((f32[128,1024]{1,0:T(8,128)}), f32[128,1024]{1,0:T(8,128)}) %all-reduce.4.cloned.1.call-update) | async-done | bytes 524304 | tf_op jit(solution)/shard_map/psum | solution.py:150
  1343.4 1.9 broadcast_multiply_fusion
  (111 shorter events, 15.3 us)
Async XLA Ops:
  7.2 10.5 copy-start.28
  7.2 10.7 copy-start.12
  11.4 8.9 collective-permute-start
  17.7 4.5 copy-start.16
  17.8 4.4 copy-start.18
  17.8 4.4 copy-start.20
  17.8 4.4 copy-start.22
  17.8 4.4 copy-start.24
  17.9 4.4 copy-start.26
  26.2 1.4 copy-start.2
  31.3 71.9 %all-to-all-start = ((f32[2,1,128,1024]{3,0,1,2:T(2,128)}), f32[2,1,128,1024]{3,0,1,2:T(2,128)S(1)}, u32[]{:S(2)}, u32[]{:S(2)}) async-start(f32[2,1,128,1024]{3,0,1,2:T(2,128)} %maximum_bitcast_fusion.4), calls=%async_computation | async-start | bytes 2097152 | tf_op jit(solution)/shard_map/all_to_all | solution.py:36
  49.4 58.9 %copy-start.10 = (f32[1,128,64,2]{1,2,0,3:T(8,128)}, f32[1,128,64,2]{1,2,0,3:T(8,128)S(1)}, u32[]{:S(2)}) copy-start(f32[1,128,64,2]{1,2,0,3:T(8,128)S(1)} %get-tuple-element.55) | copy-start | bytes 196612
  49.5 58.9 %copy-start.11 = (f32[1,128,64,2]{1,2,0,3:T(8,128)}, f32[1,128,64,2]{1,2,0,3:T(8,128)S(1)}, u32[]{:S(2)}) copy-start(f32[1,128,64,2]{1,2,0,3:T(8,128)S(1)} %get-tuple-element.56) | copy-start | bytes 196612
  115.6 193.4 %all-to-all-start.1 = ((f32[2,2,128,2,1024]{4,1,0,3,2:T(2,128)}), f32[2,2,128,2,1024]{4,1,0,3,2:T(2,128)}, u32[]{:S(2)}, u32[]{:S(2)}) async-start(f32[2,2,128,2,1024]{4,1,0,3,2:T(2,128)} %copy.68), calls=%async_computation.1 | async-start | bytes 8388608 | tf_op jit(solution)/shard_map/all_to_all | solution.py:54
  124.0 190.5 %copy-start.8 = (f32[1,2,128,128]{3,2,1,0:T(8,128)}, f32[1,2,128,128]{3,2,1,0:T(8,128)S(1)}, u32[]{:S(2)}) copy-start(f32[1,2,128,128]{3,2,1,0:T(8,128)S(1)} %get-tuple-element.50) | copy-start | bytes 393220
  124.0 190.5 %copy-start.9 = (f32[1,2,128,128]{3,2,1,0:T(8,128)}, f32[1,2,128,128]{3,2,1,0:T(8,128)S(1)}, u32[]{:S(2)}) copy-start(f32[1,2,128,128]{3,2,1,0:T(8,128)S(1)} %get-tuple-element.51) | copy-start | bytes 393220
  322.7 2.0 copy-start
  332.2 109.2 %all-to-all-start.2 = ((f32[1,2,2,128,1024]{4,1,2,0,3:T(2,128)}), f32[1,2,2,128,1024]{4,1,2,0,3:T(2,128)}, u32[]{:S(2)}, u32[]{:S(2)}) async-start(f32[1,2,2,128,1024]{4,1,2,0,3:T(2,128)} %copy.79), calls=%async_computation.2 | async-start | bytes 4194304 | tf_op jit(solution)/shard_map/all_to_all | solution.py:70
  342.9 107.1 %copy-start.13 = (f32[1,64,128]{2,1,0:T(8,128)}, f32[1,64,128]{2,1,0:T(8,128)S(1)}, u32[]{:S(2)}) copy-start(f32[1,64,128]{2,1,0:T(8,128)S(1)} %get-tuple-element.68) | copy-start | bytes 98308
  450.0 12.0 copy-start.5
  454.3 41.7 %all-to-all-start.3 = ((f32[1,64,2,1024]{3,2,0,1:T(2,128)}), f32[1,64,2,1024]{3,2,0,1:T(2,128)S(1)}, u32[]{:S(2)}, u32[]{:S(2)}) async-start(f32[1,64,2,1024]{3,2,0,1:T(2,128)} %copy.82), calls=%async_computation.3 | async-start | bytes 1048576 | tf_op jit(solution)/shard_map/all_to_all | solution.py:78
  680.3 3.6 copy-start.1
  898.8 6.0 copy-start.14
  911.2 62.2 %all-to-all-start.7 = ((f32[2,64,2,1024]{3,2,0,1:T(2,128)}), f32[2,64,2,1024]{3,2,0,1:T(2,128)}, u32[]{:S(2)}, u32[]{:S(2)}) async-start(f32[2,64,2,1024]{3,2,0,1:T(2,128)} %copy.98), calls=%async_computation.7 | async-start | bytes 2097152 | tf_op jit(solution)/shard_map/all_to_all | solution.py:78
  919.5 57.7 %copy-start.29 = (f32[1024]{0:T(1024)S(1)}, f32[1024]{0:T(1024)}, u32[]{:S(2)}) copy-start(f32[1024]{0:T(1024)} %param.12) | copy-start | bytes 12292
  919.5 57.6 %copy-start.30 = (f32[128]{0:T(128)S(1)}, f32[128]{0:T(128)}, u32[]{:S(2)}) copy-start(f32[128]{0:T(128)} %get-tuple-element.22) | copy-start | bytes 1540
  919.5 57.6 %copy-start.31 = (f32[128]{0:T(128)S(1)}, f32[128]{0:T(128)}, u32[]{:S(2)}) copy-start(f32[128]{0:T(128)} %get-tuple-element.57) | copy-start | bytes 1540
  919.5 57.6 %copy-start.32 = (f32[128]{0:T(128)S(1)}, f32[128]{0:T(128)}, u32[]{:S(2)}) copy-start(f32[128]{0:T(128)} %get-tuple-element.58) | copy-start | bytes 1540
  919.5 378.8 %all-reduce.6.cloned.1.call-start = ((), (), s32[]{:S(2)}) async-start(), calls=%async_computation.9 | async-start | bytes 229376 | tf_op jit(solution)/shard_map/psum | solution.py:151
  984.6 4.3 copy-start.3
  989.0 8.1 copy-start.7
  989.0 9.3 copy-start.6
  989.1 0.6 copy-start.15
  989.8 353.6 %all-reduce.4.cloned.1.call-start = ((), (), s32[]{:S(2)}) async-start(), calls=%async_computation.8 | async-start | bytes 1048576 | tf_op jit(solution)/shard_map/psum | solution.py:150
  992.6 8.8 collective-permute-start.1
  999.1 4.9 copy-start.4
  999.1 4.9 copy-start.17
  999.1 4.9 copy-start.19
  999.1 4.9 copy-start.21
  999.1 4.9 copy-start.23
  999.1 4.9 copy-start.25
  999.2 4.9 copy-start.27
Sparse Core Ops, SparseCore 0:
  989.9 308.3 all-reduce.5
  1301.2 42.1 all-reduce.3
where the time goes:
time: 1360 us; the launch traced here: 1350 us
  waiting for transfers between devices  759 us (56%)
  blocking collectives  350 us (26%)
  local copies, waits for them, and re-layouts  81.6 us (6%)
  starting transfers between devices  63.1 us (5%)
  other arithmetic  46.6 us (3%)
  matrix products  37.2 us (3%)
  between operations  15.3 us (1%)
    psum x1, waiting for transfers between devices, shards(): grad_short = lax.psum(short_local, ('dp', 'context')) * scale  289 us
    all_to_all x1, blocking collectives, inverse_rows(): lax.all_to_all(turned, 'context', split_axis=3, concat_axis=2, tiled=True)  196 us
    all_to_all x1, waiting for transfers between devices, forward_rows(): lax.all_to_all(turned, 'context', split_axis=2, concat_axis=3, tiled=True)  184 us
    all_to_all x1, blocking collectives, forward_rows(): lax.all_to_all(turned, 'context', split_axis=2, concat_axis=3, tiled=True)  103 us
    all_to_all x1, waiting for transfers between devices, inverse_rows(): lax.all_to_all(turned, 'context', split_axis=3, concat_axis=2, tiled=True)  98.5 us
    all_to_all x2, waiting for transfers between devices, inverse_rows(): lax.all_to_all(values, 'context', split_axis=1, concat_axis=2, tiled=True)  85 us
    all_to_all x1, waiting for transfers between devices, forward_rows(): lax.all_to_all(values.reshape(count, 1, block_len, width), 'context', spl...  53.7 us
    psum x1, waiting for transfers between devices, shards(): grad_long = lax.psum(dfilt_local, 'dp') * scale  43.4 us
  transfers between devices with their start and end apart: 9, of which 9 were waited for; matrix products, arithmetic and copies ran while one was open for 1% of the time, Pallas kernels for 0%

commit v1 on v0

--- a/solution.py
+++ b/solution.py
@@ -80,6 +80,11 @@
 
 
 def shards(q_in, k_in, v_in, short_filt, long_filt, norm_gain, grad_out):
+
+    def _use_field(array_here, dev_axis, group_axis):
+        current_block = lax.psum(lax.psum(array_here, dev_axis), group_axis)
+        return current_block
+
     block_len = q_in.shape[1]
     channels = q_in.shape[2]
     edge_rows = FILT - 1
@@ -148,7 +153,7 @@
     )
     scale = 1.0 / math.sqrt(lax.axis_size("dp") * block_len * lax.axis_size("context"))
     grad_long = lax.psum(dfilt_local, "dp") * scale
-    grad_short = lax.psum(short_local, ("dp", "context")) * scale
+    grad_short = _use_field(short_local, dev_axis="dp", group_axis="context") * scale
     return (mixed, grad_inputs.astype(jnp.bfloat16)[:, None], grad_long, grad_short)
 
 

time: 1360 us -> 1520 us (1.12)
  waiting for transfers between devices: 759 us -> 922 us
    psum x1, waiting for transfers between devices: 289 us -> 462 us  [_use_field(): current_block = lax.psum(lax.psum(array_here, dev_axis), group_axis)]
where the time goes in v1:
time: 1520 us; the launch traced here: 1510 us
  waiting for transfers between devices  922 us (61%)
  blocking collectives  350 us (23%)
  local copies, waits for them, and re-layouts  81 us (5%)
  starting transfers between devices  63 us (4%)
  other arithmetic  45.8 us (3%)
  matrix products  37.2 us (2%)
  between operations  15.3 us (1%)
    psum x1, waiting for transfers between devices, _use_field(): current_block = lax.psum(lax.psum(array_here, dev_axis), group_axis)  462 us
    all_to_all x1, blocking collectives, inverse_rows(): lax.all_to_all(turned, 'context', split_axis=3, concat_axis=2, tiled=True)  196 us
    all_to_all x1, waiting for transfers between devices, forward_rows(): lax.all_to_all(turned, 'context', split_axis=2, concat_axis=3, tiled=True)  184 us
    all_to_all x1, blocking collectives, forward_rows(): lax.all_to_all(turned, 'context', split_axis=2, concat_axis=3, tiled=True)  103 us
    all_to_all x1, waiting for transfers between devices, inverse_rows(): lax.all_to_all(turned, 'context', split_axis=3, concat_axis=2, tiled=True)  98.3 us
    all_to_all x2, waiting for transfers between devices, inverse_rows(): lax.all_to_all(values, 'context', split_axis=1, concat_axis=2, tiled=True)  85 us
    all_to_all x1, waiting for transfers between devices, forward_rows(): lax.all_to_all(values.reshape(count, 1, block_len, width), 'context', spl...  53.7 us
    all_to_all x1, blocking collectives, forward_rows(): lax.all_to_all(values.reshape(count, 1, block_len, width), 'context', spl...  40.9 us
  transfers between devices with their start and end apart: 9, of which 9 were waited for; matrix products, arithmetic and copies ran while one was open for 1% of the time, Pallas kernels for 0%

profile of v1, /device:TPU:1, one launch (start us, length us, event | category | flops | bytes accessed | tf_op | source)
XLA Modules:
  0.0 1514.1 jit_solution(16949616875394133474)
XLA Ops:
  7.2 1.4 copy.63
  8.6 1.4 copy.64
  10.0 1.4 copy.65
  11.4 6.2 collective-permute-start
  18.2 2.1 collective-permute-done
  20.3 1.9 maximum_convert_fusion
  22.3 3.9 multiply_add_fusion
  26.2 1.3 copy-done.2
  27.6 1.8 fusion.95
  29.3 1.9 maximum_bitcast_fusion.4
  31.2 17.8 %all-to-all-start = ((f32[2,1,128,1024]{3,0,1,2:T(2,128)}), f32[2,1,128,1024]{3,0,1,2:T(2,128)S(1)}, u32[]{:S(2)}, u32[]{:S(2)}) async-start(f32[2,1,128,1024]{3,0,1,2:T(2,128)} %maximum_bitcast_fusion.4), calls=%async_computation | async-start | bytes 2097152 | tf_op jit(solution)/shard_map/all_to_all | solution.py:36
  49.4 53.7 %all-to-all-done = f32[2,1,128,1024]{3,0,1,2:T(2,128)S(1)} async-done(((f32[2,1,128,1024]{3,0,1,2:T(2,128)}), f32[2,1,128,1024]{3,0,1,2:T(2,128)S(1)}, u32[]{:S(2)}, u32[]{:S(2)}) %all-to-all-start) | async-done | bytes 1048608 | tf_op jit(solution)/shard_map/all_to_all | solution.py:36
  103.1 5.2 convolution_bitcast_fusion
  108.3 7.3 copy.68
  115.6 7.8 all-to-all-start.1
  124.7 184.3 %all-to-all-done.1 = f32[2,2,128,2,1024]{4,1,0,3,2:T(2,128)} async-done(((f32[2,2,128,2,1024]{4,1,0,3,2:T(2,128)}), f32[2,2,128,2,1024]{4,1,0,3,2:T(2,128)}, u32[]{:S(2)}, u32[]{:S(2)}) %all-to-all-start.1) | async-done | bytes 4194336 | tf_op jit(solution)/shard_map/all_to_all | solution.py:54
  309.1 5.4 copy.70
  314.5 8.1 fusion.4
  322.9 1.7 copy-done
  324.6 3.3 fusion.21
  328.0 4.2 copy.79
  332.2 10.6 all-to-all-start.2
  343.0 98.3 %all-to-all-done.2 = f32[1,2,2,128,1024]{4,1,2,0,3:T(2,128)} async-done(((f32[1,2,2,128,1024]{4,1,2,0,3:T(2,128)}), f32[1,2,2,128,1024]{4,1,2,0,3:T(2,128)}, u32[]{:S(2)}, u32[]{:S(2)}) %all-to-all-start.2) | async-done | bytes 2097184 | tf_op jit(solution)/shard_map/all_to_all | solution.py:70
  441.2 2.7 copy.80
  443.9 2.2 copy.81
  446.1 3.8 reshape.785
  449.8 3.1 fusion.30
  454.1 7.8 all-to-all-start.3
  463.2 32.8 %all-to-all-done.3 = f32[1,64,2,1024]{3,2,0,1:T(2,128)S(1)} async-done(((f32[1,64,2,1024]{3,2,0,1:T(2,128)}), f32[1,64,2,1024]{3,2,0,1:T(2,128)S(1)}, u32[]{:S(2)}, u32[]{:S(2)}) %all-to-all-start.3) | async-done | bytes 524320 | tf_op jit(solution)/shard_map/all_to_all | solution.py:78
  497.1 2.2 fusion.44
  499.3 9.3 all-reduce
  509.9 1.6 squeeze_reshape.9
  511.5 3.0 fusion.48
  514.5 40.9 %all_to_all.105 = f32[1,1,128,1024]{3,0,1,2:T(1,128)} all-to-all(f32[1,1,128,1024]{3,0,1,2:T(1,128)S(1)} %fusion.48), channel_id=1, replica_groups=mesh['dp'=2,'tensor'=4,'context'=64] {'context'}, dimensions={2} | all-to-all | bytes 1048576 | tf_op jit(solution)/shard_map/all_to_all | solution.py:36
  555.3 3.1 reduce
  558.4 2.1 reshape.786
  560.6 4.3 convolution_bitcast_fusion.1
  564.8 4.2 copy.86
  569.1 103.5 %all_to_all.106 = f32[1,2,128,2,1024]{4,1,3,0,2:T(2,128)S(1)} all-to-all(f32[1,2,128,2,1024]{4,1,3,0,2:T(2,128)} %copy.86), channel_id=1, replica_groups=mesh['dp'=2,'tensor'=4,'context'=64] {'context'}, dimensions={2} | all-to-all | bytes 4194304 | tf_op jit(solution)/shard_map/all_to_all | solution.py:54
  673.6 2.5 copy.88
  676.1 4.1 copy.89
  680.3 3.6 fusion.24
  684.7 5.0 fusion.7
  689.7 7.3 copy.95
  697.0 196.5 %all_to_all.107 = f32[2,2,2,128,1024]{4,1,0,2,3:T(2,128)S(1)} all-to-all(f32[2,2,2,128,1024]{4,1,0,2,3:T(2,128)} %copy.95), channel_id=1, replica_groups=mesh['dp'=2,'tensor'=4,'context'=64] {'context'}, dimensions={3} | all-to-all | bytes 8388608 | tf_op jit(solution)/shard_map/all_to_all | solution.py:70
  893.5 5.3 copy.97
  898.8 6.0 all_to_all.95
  904.8 4.6 fusion.28
  909.4 1.8 copy.98
  911.2 8.2 all-to-all-start.7
  919.5 1.6 squeeze_reshape.7
  921.1 52.3 %all-to-all-done.7 = f32[2,64,2,1024]{3,2,0,1:T(2,128)} async-done(((f32[2,64,2,1024]{3,2,0,1:T(2,128)}), f32[2,64,2,1024]{3,2,0,1:T(2,128)}, u32[]{:S(2)}, u32[]{:S(2)}) %all-to-all-start.7) | async-done | bytes 1048608 | tf_op jit(solution)/shard_map/all_to_all | solution.py:78
  973.4 2.1 fusion.96
  975.5 1.6 squeeze.10
  977.1 7.7 fusion.41
  984.8 4.3 multiply_reduce_fusion
  989.2 1.5 pad_maximum_fusion.1
  990.7 4.4 collective-permute-start.1
  997.4 2.1 collective-permute-done.1
  999.6 2.5 pad_maximum_fusion
  1002.1 3.8 fusion.40
  1007.1 34.4 %all-reduce.7.cloned.1.call-done = (f32[128,1024]{1,0:T(8,128)}, f32[3,7,1024]{2,0,1:T(4,128)}) async-done(((f32[128,1024]{1,0:T(8,128)}, f32[3,7,1024]{2,0,1:T(4,128)}), (f32[128,1024]{1,0:T(8,128)}, f32[3,7,1024]{2,0,1:T(4,128)})) %all-reduce.7.cloned.1.call-update) | async-done | bytes 610320 | tf_op jit(solution)/shard_map/psum | solution.py:155
  1041.5 1.9 broadcast_multiply_fusion
  1043.4 461.7 %all-reduce.5.cloned.1.call-done = f32[3,7,1024]{2,0,1:T(4,128)} async-done(((f32[3,7,1024]{2,0,1:T(4,128)}), f32[3,7,1024]{2,0,1:T(4,128)}) %all-reduce.5.cloned.1.call-update) | async-done | bytes 86032 | tf_op jit(solution)/shard_map/psum | solution.py:85
  (111 shorter events, 14.4 us)
Async XLA Ops:
  7.2 10.5 copy-start.28
  7.2 10.7 copy-start.12
  11.4 8.9 collective-permute-start
  17.7 4.5 copy-start.16
  17.8 4.4 copy-start.18
  17.8 4.4 copy-start.20
  17.8 4.4 copy-start.22
  17.8 4.4 copy-start.24
  17.9 4.4 copy-start.26
  26.2 1.4 copy-start.2
  31.2 71.9 %all-to-all-start = ((f32[2,1,128,1024]{3,0,1,2:T(2,128)}), f32[2,1,128,1024]{3,0,1,2:T(2,128)S(1)}, u32[]{:S(2)}, u32[]{:S(2)}) async-start(f32[2,1,128,1024]{3,0,1,2:T(2,128)} %maximum_bitcast_fusion.4), calls=%async_computation | async-start | bytes 2097152 | tf_op jit(solution)/shard_map/all_to_all | solution.py:36
  49.4 58.9 %copy-start.10 = (f32[1,128,64,2]{1,2,0,3:T(8,128)}, f32[1,128,64,2]{1,2,0,3:T(8,128)S(1)}, u32[]{:S(2)}) copy-start(f32[1,128,64,2]{1,2,0,3:T(8,128)S(1)} %get-tuple-element.57) | copy-start | bytes 196612
  49.4 58.9 %copy-start.11 = (f32[1,128,64,2]{1,2,0,3:T(8,128)}, f32[1,128,64,2]{1,2,0,3:T(8,128)S(1)}, u32[]{:S(2)}) copy-start(f32[1,128,64,2]{1,2,0,3:T(8,128)S(1)} %get-tuple-element.58) | copy-start | bytes 196612
  115.6 193.5 %all-to-all-start.1 = ((f32[2,2,128,2,1024]{4,1,0,3,2:T(2,128)}), f32[2,2,128,2,1024]{4,1,0,3,2:T(2,128)}, u32[]{:S(2)}, u32[]{:S(2)}) async-start(f32[2,2,128,2,1024]{4,1,0,3,2:T(2,128)} %copy.68), calls=%async_computation.1 | async-start | bytes 8388608 | tf_op jit(solution)/shard_map/all_to_all | solution.py:54
  124.0 190.5 %copy-start.8 = (f32[1,2,128,128]{3,2,1,0:T(8,128)}, f32[1,2,128,128]{3,2,1,0:T(8,128)S(1)}, u32[]{:S(2)}) copy-start(f32[1,2,128,128]{3,2,1,0:T(8,128)S(1)} %get-tuple-element.52) | copy-start | bytes 393220
  124.0 190.5 %copy-start.9 = (f32[1,2,128,128]{3,2,1,0:T(8,128)}, f32[1,2,128,128]{3,2,1,0:T(8,128)S(1)}, u32[]{:S(2)}) copy-start(f32[1,2,128,128]{3,2,1,0:T(8,128)S(1)} %get-tuple-element.53) | copy-start | bytes 393220
  322.7 2.0 copy-start
  332.2 109.0 %all-to-all-start.2 = ((f32[1,2,2,128,1024]{4,1,2,0,3:T(2,128)}), f32[1,2,2,128,1024]{4,1,2,0,3:T(2,128)}, u32[]{:S(2)}, u32[]{:S(2)}) async-start(f32[1,2,2,128,1024]{4,1,2,0,3:T(2,128)} %copy.79), calls=%async_computation.2 | async-start | bytes 4194304 | tf_op jit(solution)/shard_map/all_to_all | solution.py:70
  342.9 106.9 %copy-start.13 = (f32[1,64,128]{2,1,0:T(8,128)}, f32[1,64,128]{2,1,0:T(8,128)S(1)}, u32[]{:S(2)}) copy-start(f32[1,64,128]{2,1,0:T(8,128)S(1)} %get-tuple-element.70) | copy-start | bytes 98308
  449.8 12.1 copy-start.5
  454.1 41.8 %all-to-all-start.3 = ((f32[1,64,2,1024]{3,2,0,1:T(2,128)}), f32[1,64,2,1024]{3,2,0,1:T(2,128)S(1)}, u32[]{:S(2)}, u32[]{:S(2)}) async-start(f32[1,64,2,1024]{3,2,0,1:T(2,128)} %copy.82), calls=%async_computation.3 | async-start | bytes 1048576 | tf_op jit(solution)/shard_map/all_to_all | solution.py:78
  680.3 3.7 copy-start.1
  898.8 6.1 copy-start.14
  911.2 62.2 %all-to-all-start.7 = ((f32[2,64,2,1024]{3,2,0,1:T(2,128)}), f32[2,64,2,1024]{3,2,0,1:T(2,128)}, u32[]{:S(2)}, u32[]{:S(2)}) async-start(f32[2,64,2,1024]{3,2,0,1:T(2,128)} %copy.98), calls=%async_computation.7 | async-start | bytes 2097152 | tf_op jit(solution)/shard_map/all_to_all | solution.py:78
  919.5 57.6 %copy-start.29 = (f32[1024]{0:T(1024)S(1)}, f32[1024]{0:T(1024)}, u32[]{:S(2)}) copy-start(f32[1024]{0:T(1024)} %param.12) | copy-start | bytes 12292
  919.5 57.6 %copy-start.30 = (f32[128]{0:T(128)S(1)}, f32[128]{0:T(128)}, u32[]{:S(2)}) copy-start(f32[128]{0:T(128)} %get-tuple-element.22) | copy-start | bytes 1540
  919.5 57.6 %copy-start.31 = (f32[128]{0:T(128)S(1)}, f32[128]{0:T(128)}, u32[]{:S(2)}) copy-start(f32[128]{0:T(128)} %get-tuple-element.59) | copy-start | bytes 1540
  919.5 57.6 %copy-start.32 = (f32[128]{0:T(128)S(1)}, f32[128]{0:T(128)}, u32[]{:S(2)}) copy-start(f32[128]{0:T(128)} %get-tuple-element.60) | copy-start | bytes 1540
  919.5 122.0 %all-reduce.7.cloned.1.call-start = ((), (), s32[]{:S(2)}) async-start(), calls=%async_computation.9 | async-start | bytes 1277952 | tf_op jit(solution)/shard_map/psum | solution.py:155
  984.8 4.3 copy-start.3
  989.2 6.1 copy-start.7
  989.2 7.3 copy-start.6
  990.7 8.8 collective-permute-start.1
  995.3 2.0 copy-start.15
  997.3 4.8 copy-start.17
  997.3 4.8 copy-start.19
  997.3 4.8 copy-start.21
  997.3 4.8 copy-start.23
  997.3 4.8 copy-start.25
  997.3 4.8 copy-start.27
  997.3 507.8 %all-reduce.5.cloned.1.call-start = ((), (), s32[]{:S(2)}) async-start(), calls=%async_computation.8 | async-start | bytes 229376 | tf_op jit(solution)/shard_map/psum | solution.py:85
  997.4 4.7 copy-start.4
Sparse Core Ops, SparseCore 0:
  997.4 44.0 all-reduce.6
  1044.4 460.6 all-reduce.4
